TPU v7x, 256 devices: a whole 4x4x8 slice. The times are simulated.
256 devices in a mesh: beam: 8 (over x, core), row: 32 (over y, z).
Axes of the slice: x: 4, y: 4, z: 8, core: 2. Of those that a mesh axis runs over, the one named last changes fastest.
Arguments:
- x_in: bfloat16 [4, 2, 16, 8192], P(None, None, None, 'beam'), may hold values from -6 to 6
- w_inner: bfloat16 [8192, 2, 16384], P('beam', None, 'row'), may hold values from -0.0625 to 0.0625
- w_bc: bfloat16 [8192, 2, 2048], P('beam', None, 'row'), may hold values from -0.0625 to 0.0625
- w_dt: bfloat16 [8192, 256], P('beam', 'row'), may hold values from -0.0625 to 0.0625
- conv_x_w: bfloat16 [4, 16384], P(None, 'row'), may hold values from -3 to 3
- conv_bc_w: bfloat16 [4, 2, 2048], P(None, None, 'row'), may hold values from -3 to 3
- dt_bias: float32 [256], P('row'), may hold values from -4 to 1
- a_log: float32 [256], P('row'), may hold values from 0 to 2.8
- d_skip: float32 [256], P('row'), may hold values from 0.5 to 2
- norm_gain: float32 [16384], P('row'), may hold values from 0.1 to 1.9
- w_out: bfloat16 [16384, 8192], P('row', 'beam'), may hold values from -0.046875 to 0.046875
- ssm_state: bfloat16 [2, 16, 256, 64, 256], P(None, 'beam', 'row'), may hold values from -6 to 6
- conv_x_state: bfloat16 [2, 16, 256, 64, 3], P(None, 'beam', 'row'), may hold values from -6 to 6
- conv_bc_state: bfloat16 [2, 16, 3, 2, 2048], P(None, 'beam', None, None, 'row'), may hold values from -6 to 6
- parents: int32 [4, 2, 16], replicated, may hold values from 0 to 15
Outputs:
- layer_out: bfloat16 [4, 32, 8192], P(None, 'row', 'beam')
- ssm_final: bfloat16 [2, 16, 256, 64, 256], P(None, 'beam', 'row')
- conv_x_final: bfloat16 [2, 16, 256, 64, 3], P(None, 'beam', 'row')
- conv_bc_final: bfloat16 [2, 16, 3, 2, 2048], P(None, 'beam', None, None, 'row')
All inputs are finite; a program needn't handle non-finite values.
Results may differ from a plain program's by a relative error of at most 0.0077.
Values may be sent and summed in bfloat16 or wider, within the bound.
No kernel may reach another device: no remote copies, remote signals or barrier semaphores. Data moves between devices by JAX's collectives and lax.ppermute only.
A program may use at most 64 MiB of HBM per device.

v0:
```python
import jax
import jax.numpy as jnp
from jax import lax
from jax.sharding import PartitionSpec as P

HEADS = 256
HDIM = 64
GROUPS = 8
EPS = 1e-05


def partner_2(shard, axis, stride):
    return lax.ppermute(shard, axis, [(i, i ^ 1 << stride) for i in range(lax.axis_size(axis))])


def stored(value):
    return lax.optimization_barrier(value.astype(jnp.bfloat16))


def local(
    x_in,
    w_inner,
    w_bc,
    w_dt,
    conv_x_w,
    conv_bc_w,
    dt_bias,
    a_log,
    d_skip,
    norm_gain,
    w_out,
    ssm_state,
    conv_x_state,
    conv_bc_state,
    parents,
):
    beam_index = lax.axis_index("beam")
    row_index = lax.axis_index("row")
    steps_all, sessions, width, d_local = x_in.shape
    local_beams = ssm_state.shape[1]
    heads_local = ssm_state.shape[2]
    head_dim = ssm_state.shape[3]
    tap_count = conv_x_w.shape[0]
    group_heads = HEADS // GROUPS
    group_index = row_index * heads_local // group_heads
    group_span = lax.axis_size("row") // GROUPS
    swap_rounds = group_span.bit_length() - 1
    w_inner4 = w_inner.reshape(d_local, 2, heads_local, head_dim)
    w_out3 = w_out.reshape(heads_local, head_dim, w_out.shape[1])
    conv_taps = conv_x_w.astype(jnp.float32).reshape(tap_count, heads_local, head_dim)
    gains = norm_gain.reshape(heads_local, head_dim)
    bc_taps = conv_bc_w.astype(jnp.float32)
    decay_rates = jnp.exp(a_log)
    group_mask = (jnp.arange(GROUPS, dtype=jnp.int32) == group_index).astype(jnp.float32)
    ssm_held = ssm_state
    conv_held = conv_x_state
    rim_held = conv_bc_state
    outputs = []
    for step in range(steps_all):
        parent = parents[step]
        own_parent = lax.dynamic_slice_in_dim(parent, beam_index * local_beams, local_beams, 1)
        pieces = (
            lax.all_gather(ssm_held, "beam", axis=1, tiled=True),
            lax.all_gather(conv_held, "beam", axis=1, tiled=True),
            lax.all_gather(rim_held, "beam", axis=1, tiled=True),
        )
        span_size = pieces[0].shape[1]
        beam_ids = jnp.arange(span_size, dtype=jnp.int32)
        choose = (own_parent[:, :, None] == beam_ids[None, None, :]).astype(jnp.bfloat16)
        ssm_held = jnp.einsum(
            "sij,sjhpn->sihpn", choose, pieces[0], preferred_element_type=jnp.float32
        ).astype(jnp.bfloat16)
        conv_held = jnp.einsum(
            "sij,sjhpk->sihpk", choose, pieces[1], preferred_element_type=jnp.float32
        ).astype(jnp.bfloat16)
        rim_held = jnp.einsum(
            "sij,sjkzc->sikzc", choose, pieces[2], preferred_element_type=jnp.float32
        ).astype(jnp.bfloat16)
        x_step = x_in[step]
        bc_part = jnp.einsum("sbd,dzk->sbzk", x_step, w_bc, preferred_element_type=jnp.float32)
        dt_part = jnp.einsum("sbd,dh->sbh", x_step, w_dt, preferred_element_type=jnp.float32)
        bc_sum, dt_sum = lax.psum((bc_part, dt_part), "beam")
        bc_new = stored(bc_sum)
        dt_raw = stored(dt_sum)
        bc_new = lax.dynamic_slice_in_dim(bc_new, beam_index * local_beams, local_beams, 1)
        dt_raw = lax.dynamic_slice_in_dim(dt_raw, beam_index * local_beams, local_beams, 1)
        inner_part = stored(
            lax.psum_scatter(
                jnp.einsum("sbd,dzhp->bszhp", x_step, w_inner4, preferred_element_type=jnp.float32),
                "beam",
                scatter_dimension=0,
                tiled=True,
            )
        )
        gate_in = jnp.transpose(inner_part[:, :, 0], (1, 0, 2, 3))
        x_new = jnp.transpose(inner_part[:, :, 1], (1, 0, 2, 3))
        mixed = jnp.sum(
            conv_held.astype(jnp.float32) * jnp.transpose(conv_taps[:-1], (1, 2, 0)), axis=-1
        )
        mixed = mixed + conv_taps[-1] * x_new.astype(jnp.float32)
        x_conv = stored(jax.nn.silu(mixed))
        conv_held = jnp.concatenate([conv_held[..., 1:], x_new[..., None]], axis=-1)
        mixed_bc = jnp.sum(rim_held.astype(jnp.float32) * bc_taps[:-1], axis=2) + bc_taps[
            -1
        ] * bc_new.astype(jnp.float32)
        bc_conv = stored(jax.nn.silu(mixed_bc))
        rim_held = jnp.concatenate([rim_held[:, :, 1:], bc_new[:, :, None]], axis=2)
        group_block = bc_conv
        for bit_number in range(swap_rounds):
            partner = partner_2(group_block, "row", bit_number)
            upper = jnp.bitwise_and(jnp.right_shift(row_index, bit_number), 1) == 1
            group_block = jnp.where(
                upper,
                jnp.concatenate([partner, group_block], axis=3),
                jnp.concatenate([group_block, partner], axis=3),
            )
        bc_group = group_block.astype(jnp.float32)
        b_in = bc_group[:, :, 0]
        c_out = bc_group[:, :, 1]
        step_size = jax.nn.softplus(dt_raw.astype(jnp.float32) + dt_bias)
        decay = jnp.exp(-decay_rates * step_size)
        x_val = x_conv.astype(jnp.float32)
        state = (
            decay[..., None, None] * ssm_held.astype(jnp.float32)
            + (step_size[..., None] * x_val)[..., None] * b_in[:, :, None, None, :]
        )
        read = jnp.sum(state * c_out[:, :, None, None, :], axis=-1) + d_skip[:, None] * x_val
        ssm_held = stored(state)
        gated = read * jax.nn.silu(gate_in.astype(jnp.float32))
        square_sum = jnp.sum(gated * gated, axis=(2, 3))
        stat_terms = square_sum[..., None] * group_mask
        totals = lax.psum(stat_terms, "row")
        mean_sq = lax.dynamic_index_in_dim(totals, group_index, 2, keepdims=False) / (
            group_heads * HDIM
        )
        normed = stored(gated * lax.rsqrt(mean_sq + EPS)[..., None, None] * gains)
        partial_out = jnp.einsum(
            "sbhp,hpd->sbd",
            lax.all_gather(normed, "beam", axis=1, tiled=True),
            w_out3,
            preferred_element_type=jnp.float32,
        )
        flat_rows = partial_out.reshape(sessions * width, partial_out.shape[2])
        outputs.append(
            lax.psum_scatter(flat_rows, "row", scatter_dimension=0, tiled=True).astype(jnp.bfloat16)
        )
    return (jnp.stack(outputs), ssm_held, conv_held, rim_held)


def solution(mesh):
    placed = (
        P(None, None, None, "beam"),
        P("beam", None, "row"),
        P("beam", None, "row"),
        P("beam", "row"),
        P(None, "row"),
        P(None, None, "row"),
        P("row"),
        P("row"),
        P("row"),
        P("row"),
        P("row", "beam"),
        P(None, "beam", "row", None, None),
        P(None, "beam", "row", None, None),
        P(None, "beam", None, None, "row"),
        P(),
    )
    return jax.shard_map(
        local,
        mesh=mesh,
        in_specs=placed,
        out_specs=(
            P(None, "row", "beam"),
            P(None, "beam", "row", None, None),
            P(None, "beam", "row", None, None),
            P(None, "beam", None, None, "row"),
        ),
        check_vma=False,
    )
```

profile of v0, /device:TPU:4, one launch (start us, length us, event | category | flops | bytes accessed | tf_op | source)
XLA Modules:
  0.0 760.4 jit_solution(5823953862466214772)
XLA Ops:
  7.2 4.8 copy.199
  24.1 22.1 %all-reduce.6 = (bf16[2,16,2,64]{3,1,2,0:T(8,128)(2,1)S(1)}, bf16[2,16,2,64]{3,1,2,0:T(8,128)(2,1)S(1)}, bf16[2,16,2,64]{3,1,2,0:T(8,128)(2,1)S(1)}, bf16[2,16,8...) all-reduce(f32[2,16,2,64]{3,1,2,0:T(8,128)S(1)} %fusion.30, ...), channel_id=1, replica_groups=mesh['beam'=8,'row'=32] {'beam'}, use_global_device_ids=true, to_apply=%region_22.23 | all-reduce | flops 17408 | bytes 104448 | tf_op jit(solution)/shard_map/psum | solution.py:82
  46.3 16.7 %all_gather.50 = bf16[2,16,3,2,64]{4,3,2,0,1:T(2,128)(2,1)S(1)} all-gather(bf16[2,2,3,2,64]{4,3,2,0,1:T(2,128)(2,1)S(1)} %copy.204), channel_id=1, replica_groups=mesh['beam'=8,'row'=32] {'beam'}, dimensions={1}, use_global_device_ids=true | all-gather | bytes 27648 | tf_op jit(solution)/shard_map/all_gather | solution.py:65
  63.3 12.8 %all_gather.54 = bf16[2,16,3,2,64]{4,3,2,0,1:T(2,128)(2,1)S(1)} all-gather(bf16[2,2,3,2,64]{4,3,2,0,1:T(2,128)(2,1)S(1)} %copy.220), channel_id=1, replica_groups=mesh['beam'=8,'row'=32] {'beam'}, dimensions={1}, use_global_device_ids=true | all-gather | bytes 27648 | tf_op jit(solution)/shard_map/all_gather | solution.py:65
  76.5 12.8 %all_gather.58 = bf16[2,16,3,2,64]{4,3,2,0,1:T(2,128)(2,1)S(1)} all-gather(bf16[2,2,3,2,64]{4,3,2,0,1:T(2,128)(2,1)S(1)} %copy.236), channel_id=1, replica_groups=mesh['beam'=8,'row'=32] {'beam'}, dimensions={1}, use_global_device_ids=true | all-gather | bytes 27648 | tf_op jit(solution)/shard_map/all_gather | solution.py:65
  89.6 12.8 %all_gather.62 = bf16[2,16,3,2,64]{4,3,2,0,1:T(2,128)(2,1)S(1)} all-gather(bf16[2,2,3,2,64]{4,3,2,0,1:T(2,128)(2,1)S(1)} %copy.252), channel_id=1, replica_groups=mesh['beam'=8,'row'=32] {'beam'}, dimensions={1}, use_global_device_ids=true | all-gather | bytes 27648 | tf_op jit(solution)/shard_map/all_gather | solution.py:65
  104.6 12.8 %all_gather.49 = bf16[2,16,8,64,3]{3,2,4,0,1:T(8,128)(2,1)S(1)} all-gather(bf16[2,2,8,64,3]{3,2,4,0,1:T(8,128)(2,1)S(1)} %copy.196), channel_id=1, replica_groups=mesh['beam'=8,'row'=32] {'beam'}, dimensions={1}, use_global_device_ids=true | all-gather | bytes 110592 | tf_op jit(solution)/shard_map/all_gather | solution.py:64
  124.4 12.8 %all_gather.53 = bf16[2,16,8,64,3]{3,2,4,0,1:T(8,128)(2,1)S(1)} all-gather(bf16[2,2,8,64,3]{3,2,4,0,1:T(8,128)(2,1)S(1)} %copy.214), channel_id=1, replica_groups=mesh['beam'=8,'row'=32] {'beam'}, dimensions={1}, use_global_device_ids=true | all-gather | bytes 110592 | tf_op jit(solution)/shard_map/all_gather | solution.py:64
  138.4 12.8 %all_gather.57 = bf16[2,16,8,64,3]{3,2,4,0,1:T(8,128)(2,1)S(1)} all-gather(bf16[2,2,8,64,3]{3,2,4,0,1:T(8,128)(2,1)S(1)} %copy.230), channel_id=1, replica_groups=mesh['beam'=8,'row'=32] {'beam'}, dimensions={1}, use_global_device_ids=true | all-gather | bytes 110592 | tf_op jit(solution)/shard_map/all_gather | solution.py:64
  152.2 14.6 %all_gather.61 = bf16[2,16,8,64,3]{3,2,4,0,1:T(8,128)(2,1)S(1)} all-gather(bf16[2,2,8,64,3]{3,2,4,0,1:T(8,128)(2,1)S(1)} %copy.246), channel_id=1, replica_groups=mesh['beam'=8,'row'=32] {'beam'}, dimensions={1}, use_global_device_ids=true | all-gather | bytes 110592 | tf_op jit(solution)/shard_map/all_gather | solution.py:64
  167.4 39.3 %all-gather.5.cloned.1.call-done = bf16[2,16,8,64,256]{4,3,2,0,1:T(8,128)(2,1)} async-done(((bf16[2,2,8,64,256]{4,3,2,0,1:T(8,128)(2,1)}), bf16[2,16,8,64,256]{4,3,2,0,1:T(8,128)(2,1)}) %all-gather.5.cloned.1.call-update) | async-done | bytes 8388624 | tf_op jit(solution)/shard_map/all_gather | solution.py:63
  206.7 10.6 %multiply_reduce_fusion.3 = (f32[2,2,8,64]{1,3,2,0:T(8,128)S(1)}, bf16[2,2,8,64,256]{4,1,3,2,0:T(2,128)(2,1)S(1)}) fusion(f32[2,2,256]{2,1,0:T(2,128)S(1)} %get-tuple-element.64, f32[2,2,256]{2,1,0:T(2,128)S(1)} %get-tuple-element.65, f32[2,2,8,64]{1,3,2,0:T(8,128)S(1)} %copy.203, bf16[2,16,8,64,256]{4,3,2,0,1:T(8,128)(2,1)} %all-gather.5.cloned.1.call-done, ...), kind=kOutput, calls=%fused_computation.14 | convolution fusion | flops 20969536 | bytes 9461904 | tf_op jit(solution)/shard_map/sij,sjhpn->sihpn/dot_general | solution.py:70
  227.2 44.0 %all-gather.7.cloned.1.call-done = bf16[2,16,8,64,256]{4,3,2,0,1:T(8,128)(2,1)} async-done(((bf16[2,2,8,64,256]{4,3,2,0,1:T(8,128)(2,1)}), bf16[2,16,8,64,256]{4,3,2,0,1:T(8,128)(2,1)}) %all-gather.7.cloned.1.call-update) | async-done | bytes 8388624 | tf_op jit(solution)/shard_map/all_gather | solution.py:63
  271.2 10.6 %multiply_reduce_fusion.2 = (f32[2,2,8,64]{1,3,2,0:T(8,128)S(1)}, bf16[2,2,8,64,256]{4,1,3,2,0:T(2,128)(2,1)S(1)}) fusion(f32[2,2,256]{2,1,0:T(2,128)S(1)} %get-tuple-element.66, f32[2,2,256]{2,1,0:T(2,128)S(1)} %get-tuple-element.67, f32[2,2,8,64]{1,3,2,0:T(8,128)S(1)} %copy.219, bf16[2,16,8,64,256]{4,3,2,0,1:T(8,128)(2,1)} %all-gather.7.cloned.1.call-done, ...), kind=kOutput, calls=%fused_computation.12 | convolution fusion | flops 20969536 | bytes 9461904 | tf_op jit(solution)/shard_map/sij,sjhpn->sihpn/dot_general | solution.py:70
  291.8 43.8 %all-gather.9.cloned.1.call-done = bf16[2,16,8,64,256]{4,3,2,0,1:T(8,128)(2,1)} async-done(((bf16[2,2,8,64,256]{4,3,2,0,1:T(8,128)(2,1)}), bf16[2,16,8,64,256]{4,3,2,0,1:T(8,128)(2,1)}) %all-gather.9.cloned.1.call-update) | async-done | bytes 8388624 | tf_op jit(solution)/shard_map/all_gather | solution.py:63
  335.6 10.6 %multiply_reduce_fusion.1 = (f32[2,2,8,64]{1,3,2,0:T(8,128)S(1)}, bf16[2,2,8,64,256]{4,1,3,2,0:T(2,128)(2,1)S(1)}) fusion(f32[2,2,256]{2,1,0:T(2,128)S(1)} %get-tuple-element.68, f32[2,2,256]{2,1,0:T(2,128)S(1)} %get-tuple-element.69, f32[2,2,8,64]{1,3,2,0:T(8,128)S(1)} %copy.235, bf16[2,16,8,64,256]{4,3,2,0,1:T(8,128)(2,1)} %all-gather.9.cloned.1.call-done, ...), kind=kOutput, calls=%fused_computation.10 | convolution fusion | flops 20969536 | bytes 9461904 | tf_op jit(solution)/shard_map/sij,sjhpn->sihpn/dot_general | solution.py:70
  357.5 42.7 %all-gather.11.cloned.1.call-done = bf16[2,16,8,64,256]{4,3,2,0,1:T(8,128)(2,1)} async-done(((bf16[2,2,8,64,256]{4,3,2,0,1:T(8,128)(2,1)}), bf16[2,16,8,64,256]{4,3,2,0,1:T(8,128)(2,1)}) %all-gather.11.cloned.1.call-update) | async-done | bytes 8388624 | tf_op jit(solution)/shard_map/all_gather | solution.py:63
  400.1 10.6 %fusion.172 = (bf16[2,2,8,64,256]{4,1,3,2,0:T(2,128)(2,1)S(1)}, f32[2,2,8,64]{1,3,2,0:T(8,128)S(1)}) fusion(f32[2,2,256]{2,1,0:T(2,128)S(1)} %get-tuple-element.70, f32[2,2,256]{2,1,0:T(2,128)S(1)} %get-tuple-element.71, f32[2,2,8,64]{1,3,2,0:T(8,128)S(1)} %copy.251, bf16[2,16,8,64,256]{4,3,2,0,1:T(8,128)(2,1)} %all-gather.11.cloned.1.call-done, ...), kind=kOutput, calls=%fused_computation.290 | convolution fusion | flops 20969536 | bytes 9461904 | tf_op jit(solution)/shard_map/sij,sjhpn->sihpn/dot_general | solution.py:70
  411.3 143.4 %all-reduce.5 = (f32[2,2,8]{1,0,2:T(2,128)S(1)}, f32[2,2,8]{1,0,2:T(2,128)S(1)}, f32[2,2,8]{1,0,2:T(2,128)S(1)}, f32[2,2,8]{1,0,2:T(2,128)S(1)}) all-reduce(f32[2,2,8]{1,0,2:T(2,128)S(1)} %get-tuple-element.105, f32[2,2,8]{1,0,2:T(2,128)S(1)} %get-tuple-element.104, ...), channel_id=1, replica_groups=mesh['beam'=8,'row'=32] {'row'}, use_global_device_ids=true, to_apply=%region_34.35 | all-reduce | flops 128 | bytes 1024 | tf_op jit(solution)/shard_map/psum | solution.py:132
  554.8 12.3 %all_gather.63 = bf16[2,16,8,64]{3,2,0,1:T(8,128)(2,1)S(1)} all-gather(bf16[2,2,8,64]{3,2,0,1:T(8,128)(2,1)S(1)} %copy.255), channel_id=1, replica_groups=mesh['beam'=8,'row'=32] {'beam'}, dimensions={1}, use_global_device_ids=true | all-gather | bytes 36864 | tf_op jit(solution)/shard_map/all_gather | solution.py:139
  567.4 12.7 %all_gather.59 = bf16[2,16,8,64]{3,2,0,1:T(8,128)(2,1)S(1)} all-gather(bf16[2,2,8,64]{3,2,0,1:T(8,128)(2,1)S(1)} %copy.239), channel_id=1, replica_groups=mesh['beam'=8,'row'=32] {'beam'}, dimensions={1}, use_global_device_ids=true | all-gather | bytes 36864 | tf_op jit(solution)/shard_map/all_gather | solution.py:139
  580.5 12.7 %all_gather.55 = bf16[2,16,8,64]{3,2,0,1:T(8,128)(2,1)S(1)} all-gather(bf16[2,2,8,64]{3,2,0,1:T(8,128)(2,1)S(1)} %copy.223), channel_id=1, replica_groups=mesh['beam'=8,'row'=32] {'beam'}, dimensions={1}, use_global_device_ids=true | all-gather | bytes 36864 | tf_op jit(solution)/shard_map/all_gather | solution.py:139
  593.6 12.7 %all_gather.51 = bf16[2,16,8,64]{3,2,0,1:T(8,128)(2,1)S(1)} all-gather(bf16[2,2,8,64]{3,2,0,1:T(8,128)(2,1)S(1)} %copy.207), channel_id=1, replica_groups=mesh['beam'=8,'row'=32] {'beam'}, dimensions={1}, use_global_device_ids=true | all-gather | bytes 36864 | tf_op jit(solution)/shard_map/all_gather | solution.py:139
  606.7 142.2 %all-reduce.8 = (bf16[32,1024]{1,0:T(8,128)(2,1)S(1)}, bf16[32,1024]{1,0:T(8,128)(2,1)S(1)}, bf16[32,1024]{1,0:T(8,128)(2,1)S(1)}, bf16[32,1024]{1,0:T(8,128)(2,1)S(1)}) all-reduce(f32[32,1024]{1,0:T(8,128)S(1)} %convolution_bitcast_fusion.4, ...), channel_id=9, replica_groups=mesh['beam'=8,'row'=32] {'row'}, use_global_device_ids=true, to_apply=%region_35.36.clone | all-reduce | flops 131072 | bytes 786432
  (206 shorter events, 61.9 us)
Async XLA Ops:
  7.2 559.9 %copy-start = (bf16[512,1024]{1,0:T(8,128)(2,1)S(1)}, bf16[512,1024]{1,0:T(8,128)(2,1)}, u32[]{:S(2)}) copy-start(bf16[512,1024]{1,0:T(8,128)(2,1)} %param.25) | copy-start | bytes 3145732
  7.2 115.6 %reduce-scatter.5.cloned.1.call-start = ((), (), s32[]{:S(2)}) async-start(), calls=%async_computation.5 | async-start | bytes 294912 | tf_op jit(solution)/shard_map/reduce_scatter | solution.py:88
  14.0 109.6 %reduce-scatter.7.cloned.1.call-start = ((), (), s32[]{:S(2)}) async-start(), calls=%async_computation.7 | async-start | bytes 294912 | tf_op jit(solution)/shard_map/reduce_scatter | solution.py:88
  15.9 121.6 %reduce-scatter.9.cloned.1.call-start = ((), (), s32[]{:S(2)}) async-start(), calls=%async_computation.9 | async-start | bytes 294912 | tf_op jit(solution)/shard_map/reduce_scatter | solution.py:88
  17.9 133.6 %reduce-scatter.11.cloned.1.call-start = ((), (), s32[]{:S(2)}) async-start(), calls=%async_computation.11 | async-start | bytes 294912 | tf_op jit(solution)/shard_map/reduce_scatter | solution.py:88
  19.9 26.4 %copy-start.6 = (bf16[2,2,3,2,64]{4,3,2,1,0:T(2,128)(2,1)S(1)}, bf16[2,2,3,2,64]{4,3,2,1,0:T(2,128)(2,1)}, u32[]{:S(2)}) copy-start(bf16[2,2,3,2,64]{4,3,2,1,0:T(2,128)(2,1)} %param.28) | copy-start | bytes 9220
  19.9 186.9 %all-gather.5.cloned.1.call-start = ((), (), s32[]{:S(2)}) async-start(), calls=%async_computation.4 | async-start | bytes 9437184 | tf_op jit(solution)/shard_map/all_gather | solution.py:63
  22.2 40.7 %copy-start.7 = (s32[4,2,16]{2,1,0:T(2,128)S(1)}, s32[4,2,16]{2,1,0:T(2,128)}, u32[]{:S(2)}) copy-start(s32[4,2,16]{2,1,0:T(2,128)} %param.29) | copy-start | bytes 1540
  22.2 82.3 %copy-start.4 = (bf16[2,2,8,64,3]{3,2,4,1,0:T(8,128)(2,1)S(1)}, bf16[2,2,8,64,3]{3,2,4,1,0:T(8,128)(2,1)}, u32[]{:S(2)}) copy-start(bf16[2,2,8,64,3]{3,2,4,1,0:T(8,128)(2,1)} %param.27) | copy-start | bytes 36868
  22.2 95.1 %copy-start.12 = (f32[8]{0:T(128)S(1)}, f32[8]{0:T(128)}, u32[]{:S(2)}) copy-start(f32[8]{0:T(128)} %param.22) | copy-start | bytes 100
  22.2 95.3 %copy-start.9 = (f32[8]{0:T(128)S(1)}, f32[8]{0:T(128)}, u32[]{:S(2)}) copy-start(f32[8]{0:T(128)} %param.21) | copy-start | bytes 100
  22.2 95.5 %copy-start.3 = (bf16[4,512]{1,0:T(4,128)(2,1)S(1)}, bf16[4,512]{1,0:T(4,128)(2,1)}, u32[]{:S(2)}) copy-start(bf16[4,512]{1,0:T(4,128)(2,1)} %param.19) | copy-start | bytes 12292
  22.3 248.9 %all-gather.7.cloned.1.call-start = ((), (), s32[]{:S(2)}) async-start(), calls=%async_computation.6 | async-start | bytes 9437184 | tf_op jit(solution)/shard_map/all_gather | solution.py:63
  102.8 15.0 %collective-permute-start = (bf16[2,2,2,64]{3,1,2,0:T(2,128)(2,1)S(1)}, bf16[2,2,2,64]{3,1,2,0:T(2,128)(2,1)S(1)}, u32[]{:S(2)}, u32[]{:S(2)}) collective-permute-start(bf16[2,2,2,64]{3,1,2,0:T(2,128)(2,1)S(1)} %get-tuple-element.101), channel_id=1, source_target_pairs={{0,1},{1,0},{2,3},{3,2},{4,5},{5,4},{6,7},{7,6},{8,9},{9,8},{10,11... | collective-permute-start | bytes 3080 | tf_op jit(solution)/shard_map/ppermute | solution.py:13
  117.8 4.9 collective-permute-start.1
  218.6 117.1 %all-gather.9.cloned.1.call-start = ((), (), s32[]{:S(2)}) async-start(), calls=%async_computation.8 | async-start | bytes 9437184 | tf_op jit(solution)/shard_map/all_gather | solution.py:63
  218.6 3.7 collective-permute-start.2
  222.4 4.5 collective-permute-start.3
  283.0 117.1 %all-gather.11.cloned.1.call-start = ((), (), s32[]{:S(2)}) async-start(), calls=%async_computation.10 | async-start | bytes 9437184 | tf_op jit(solution)/shard_map/all_gather | solution.py:63
  283.1 3.8 collective-permute-start.4
  287.0 4.5 collective-permute-start.5
  347.5 3.7 collective-permute-start.6
  351.2 4.5 collective-permute-start.7
  400.1 10.8 %copy-start.10 = (f32[8]{0:T(128)S(1)}, f32[8]{0:T(128)}, u32[]{:S(2)}) copy-start(f32[8]{0:T(128)} %param.23) | copy-start | bytes 100
  (6 other events, 31.7 us)
Sparse Core Ops, SparseCore 0:
  14.1 30.9 reduce-scatter.4
  47.8 31.9 reduce-scatter.6
  82.3 31.9 reduce-scatter.8
  116.8 32.1 reduce-scatter.10
  151.3 55.4 all-gather.4
  218.7 52.4 all-gather.6
  283.1 52.4 all-gather.8
  347.6 52.4 all-gather.10
where the time goes:
time: 769 us; the launch traced here: 760 us
  blocking collectives  466 us (61%)
  waiting for transfers between devices  182 us (24%)
  matrix products  51.5 us (7%)
  local copies, waits for them, and re-layouts  25.6 us (3%)
  starting transfers between devices  18.3 us (2%)
  between operations  15 us (2%)
    all_gather x4, waiting for transfers between devices, local(): lax.all_gather(ssm_held, 'beam', axis=1, tiled=True)  170 us
    psum x1, blocking collectives, local(): totals = lax.psum(stat_terms, 'row')  143 us
    unnamed x1, blocking collectives  142 us
    all_gather x4, blocking collectives, local(): lax.all_gather(rim_held, 'beam', axis=1, tiled=True)  55.1 us
    all_gather x4, blocking collectives, local(): lax.all_gather(conv_held, 'beam', axis=1, tiled=True)  52.9 us
    all_gather x4, blocking collectives, local(): lax.all_gather(normed, 'beam', axis=1, tiled=True)  50.6 us
    dot_general x4, matrix products, local(): jnp.einsum('sij,sjhpn->sihpn', choose, pieces[0], preferred_element_type=...  42.5 us
    psum x1, blocking collectives, local(): bc_sum, dt_sum = lax.psum((bc_part, dt_part), 'beam')  22.1 us
  transfers between devices with their start and end apart: 16, of which 11 were waited for; matrix products, arithmetic and copies ran while one was open for 3% of the time, Pallas kernels for 0%

commit v1 on v0

--- a/solution.py
+++ b/solution.py
@@ -129,7 +129,7 @@
         gated = read * jax.nn.silu(gate_in.astype(jnp.float32))
         square_sum = jnp.sum(gated * gated, axis=(2, 3))
         stat_terms = square_sum[..., None] * group_mask
-        totals = lax.psum(stat_terms, "row")
+        totals = jnp.sum(lax.all_gather(stat_terms, "row"), axis=0)
         mean_sq = lax.dynamic_index_in_dim(totals, group_index, 2, keepdims=False) / (
             group_heads * HDIM
         )

time: 769 us -> 819 us (1.065)
  blocking collectives: 466 us -> 517 us
    all_gather x0 -> x4, blocking collectives: none -> 191 us  [local(): totals = jnp.sum(lax.all_gather(stat_terms, 'row'), axis=0)]
    psum x1 -> x0, blocking collectives: 143 us -> none  [local(): totals = lax.psum(stat_terms, 'row')]
  transfers between devices with their start and end apart: 16 -> 16, of which waited for: 11 -> 11; matrix products, arithmetic and copies ran while one was open for 3% -> 2% of each run, Pallas kernels for 0% -> 0%
where the time goes in v1:
time: 819 us; the launch traced here: 811 us
  blocking collectives  517 us (63%)
  waiting for transfers between devices  182 us (22%)
  matrix products  51.4 us (6%)
  local copies, waits for them, and re-layouts  24.3 us (3%)
  starting transfers between devices  18.3 us (2%)
  between operations  15 us (2%)
    all_gather x4, blocking collectives, local(): totals = jnp.sum(lax.all_gather(stat_terms, 'row'), axis=0)  191 us
    all_gather x4, waiting for transfers between devices, local(): lax.all_gather(ssm_held, 'beam', axis=1, tiled=True)  170 us
    unnamed x1, blocking collectives  145 us
    all_gather x4, blocking collectives, local(): lax.all_gather(rim_held, 'beam', axis=1, tiled=True)  55.1 us
    all_gather x4, blocking collectives, local(): lax.all_gather(conv_held, 'beam', axis=1, tiled=True)  52.9 us
    all_gather x4, blocking collectives, local(): lax.all_gather(normed, 'beam', axis=1, tiled=True)  50.5 us
    dot_general x4, matrix products, local(): jnp.einsum('sij,sjhpn->sihpn', choose, pieces[0], preferred_element_type=...  42.5 us
    psum x1, blocking collectives, local(): bc_sum, dt_sum = lax.psum((bc_part, dt_part), 'beam')  22.1 us
  transfers between devices with their start and end apart: 16, of which 11 were waited for; matrix products, arithmetic and copies ran while one was open for 2% of the time, Pallas kernels for 0%

profile of v1, /device:TPU:4, one launch (start us, length us, event | category | flops | bytes accessed | tf_op | source)
XLA Modules:
  0.0 810.7 jit_solution(11728638845253773270)
XLA Ops:
  24.1 22.1 %all-reduce.5 = (bf16[2,16,2,64]{3,1,2,0:T(8,128)(2,1)S(1)}, bf16[2,16,2,64]{3,1,2,0:T(8,128)(2,1)S(1)}, bf16[2,16,2,64]{3,1,2,0:T(8,128)(2,1)S(1)}, bf16[2,16,8...) all-reduce(f32[2,16,2,64]{3,1,2,0:T(8,128)S(1)} %fusion.30, ...), channel_id=1, replica_groups=mesh['beam'=8,'row'=32] {'beam'}, use_global_device_ids=true, to_apply=%region_22.23 | all-reduce | flops 17408 | bytes 104448 | tf_op jit(solution)/shard_map/psum | solution.py:82
  46.3 16.7 %all_gather.66 = bf16[2,16,3,2,64]{4,3,2,0,1:T(2,128)(2,1)S(1)} all-gather(bf16[2,2,3,2,64]{4,3,2,0,1:T(2,128)(2,1)S(1)} %copy.324), channel_id=1, replica_groups=mesh['beam'=8,'row'=32] {'beam'}, dimensions={1}, use_global_device_ids=true | all-gather | bytes 27648 | tf_op jit(solution)/shard_map/all_gather | solution.py:65
  63.3 12.8 %all_gather.71 = bf16[2,16,3,2,64]{4,3,2,0,1:T(2,128)(2,1)S(1)} all-gather(bf16[2,2,3,2,64]{4,3,2,0,1:T(2,128)(2,1)S(1)} %copy.340), channel_id=1, replica_groups=mesh['beam'=8,'row'=32] {'beam'}, dimensions={1}, use_global_device_ids=true | all-gather | bytes 27648 | tf_op jit(solution)/shard_map/all_gather | solution.py:65
  76.5 12.8 %all_gather.76 = bf16[2,16,3,2,64]{4,3,2,0,1:T(2,128)(2,1)S(1)} all-gather(bf16[2,2,3,2,64]{4,3,2,0,1:T(2,128)(2,1)S(1)} %copy.356), channel_id=1, replica_groups=mesh['beam'=8,'row'=32] {'beam'}, dimensions={1}, use_global_device_ids=true | all-gather | bytes 27648 | tf_op jit(solution)/shard_map/all_gather | solution.py:65
  89.6 12.8 %all_gather.81 = bf16[2,16,3,2,64]{4,3,2,0,1:T(2,128)(2,1)S(1)} all-gather(bf16[2,2,3,2,64]{4,3,2,0,1:T(2,128)(2,1)S(1)} %copy.372), channel_id=1, replica_groups=mesh['beam'=8,'row'=32] {'beam'}, dimensions={1}, use_global_device_ids=true | all-gather | bytes 27648 | tf_op jit(solution)/shard_map/all_gather | solution.py:65
  104.6 12.8 %all_gather.65 = bf16[2,16,8,64,3]{3,2,4,0,1:T(8,128)(2,1)S(1)} all-gather(bf16[2,2,8,64,3]{3,2,4,0,1:T(8,128)(2,1)S(1)} %copy.316), channel_id=1, replica_groups=mesh['beam'=8,'row'=32] {'beam'}, dimensions={1}, use_global_device_ids=true | all-gather | bytes 110592 | tf_op jit(solution)/shard_map/all_gather | solution.py:64
  124.4 12.8 %all_gather.70 = bf16[2,16,8,64,3]{3,2,4,0,1:T(8,128)(2,1)S(1)} all-gather(bf16[2,2,8,64,3]{3,2,4,0,1:T(8,128)(2,1)S(1)} %copy.334), channel_id=1, replica_groups=mesh['beam'=8,'row'=32] {'beam'}, dimensions={1}, use_global_device_ids=true | all-gather | bytes 110592 | tf_op jit(solution)/shard_map/all_gather | solution.py:64
  138.4 12.8 %all_gather.75 = bf16[2,16,8,64,3]{3,2,4,0,1:T(8,128)(2,1)S(1)} all-gather(bf16[2,2,8,64,3]{3,2,4,0,1:T(8,128)(2,1)S(1)} %copy.350), channel_id=1, replica_groups=mesh['beam'=8,'row'=32] {'beam'}, dimensions={1}, use_global_device_ids=true | all-gather | bytes 110592 | tf_op jit(solution)/shard_map/all_gather | solution.py:64
  152.2 14.6 %all_gather.80 = bf16[2,16,8,64,3]{3,2,4,0,1:T(8,128)(2,1)S(1)} all-gather(bf16[2,2,8,64,3]{3,2,4,0,1:T(8,128)(2,1)S(1)} %copy.366), channel_id=1, replica_groups=mesh['beam'=8,'row'=32] {'beam'}, dimensions={1}, use_global_device_ids=true | all-gather | bytes 110592 | tf_op jit(solution)/shard_map/all_gather | solution.py:64
  167.4 39.3 %all-gather.5.cloned.1.call-done = bf16[2,16,8,64,256]{4,3,2,0,1:T(8,128)(2,1)} async-done(((bf16[2,2,8,64,256]{4,3,2,0,1:T(8,128)(2,1)}), bf16[2,16,8,64,256]{4,3,2,0,1:T(8,128)(2,1)}) %all-gather.5.cloned.1.call-update) | async-done | bytes 8388624 | tf_op jit(solution)/shard_map/all_gather | solution.py:63
  227.2 44.0 %all-gather.7.cloned.1.call-done = bf16[2,16,8,64,256]{4,3,2,0,1:T(8,128)(2,1)} async-done(((bf16[2,2,8,64,256]{4,3,2,0,1:T(8,128)(2,1)}), bf16[2,16,8,64,256]{4,3,2,0,1:T(8,128)(2,1)}) %all-gather.7.cloned.1.call-update) | async-done | bytes 8388624 | tf_op jit(solution)/shard_map/all_gather | solution.py:63
  271.2 10.6 %multiply_reduce_fusion.2 = (f32[2,2,8,64]{1,3,2,0:T(8,128)S(1)}, bf16[2,2,8,64,256]{4,1,3,2,0:T(2,128)(2,1)S(1)}) fusion(f32[2,2,256]{2,1,0:T(2,128)S(1)} %get-tuple-element.70, f32[2,2,256]{2,1,0:T(2,128)S(1)} %get-tuple-element.71, f32[2,2,8,64]{1,3,2,0:T(8,128)S(1)} %copy.339, bf16[2,16,8,64,256]{4,3,2,0,1:T(8,128)(2,1)} %all-gather.7.cloned.1.call-done, ...), kind=kOutput, calls=%fused_computation.12 | convolution fusion | flops 20969536 | bytes 9461904 | tf_op jit(solution)/shard_map/sij,sjhpn->sihpn/dot_general | solution.py:70
  291.8 43.8 %all-gather.9.cloned.1.call-done = bf16[2,16,8,64,256]{4,3,2,0,1:T(8,128)(2,1)} async-done(((bf16[2,2,8,64,256]{4,3,2,0,1:T(8,128)(2,1)}), bf16[2,16,8,64,256]{4,3,2,0,1:T(8,128)(2,1)}) %all-gather.9.cloned.1.call-update) | async-done | bytes 8388624 | tf_op jit(solution)/shard_map/all_gather | solution.py:63
  357.5 42.7 %all-gather.11.cloned.1.call-done = bf16[2,16,8,64,256]{4,3,2,0,1:T(8,128)(2,1)} async-done(((bf16[2,2,8,64,256]{4,3,2,0,1:T(8,128)(2,1)}), bf16[2,16,8,64,256]{4,3,2,0,1:T(8,128)(2,1)}) %all-gather.11.cloned.1.call-update) | async-done | bytes 8388624 | tf_op jit(solution)/shard_map/all_gather | solution.py:63
  400.1 10.6 %fusion.172 = (bf16[2,2,8,64,256]{4,1,3,2,0:T(2,128)(2,1)S(1)}, f32[2,2,8,64]{1,3,2,0:T(8,128)S(1)}) fusion(f32[2,2,256]{2,1,0:T(2,128)S(1)} %get-tuple-element.74, f32[2,2,256]{2,1,0:T(2,128)S(1)} %get-tuple-element.75, f32[2,2,8,64]{1,3,2,0:T(8,128)S(1)} %copy.371, bf16[2,16,8,64,256]{4,3,2,0,1:T(8,128)(2,1)} %all-gather.11.cloned.1.call-done, ...), kind=kOutput, calls=%fused_computation.290 | convolution fusion | flops 20969536 | bytes 9461904 | tf_op jit(solution)/shard_map/sij,sjhpn->sihpn/dot_general | solution.py:70
  411.2 49.9 %all_gather.67 = f32[32,2,2,8]{3,2,1,0:T(2,128)S(1)} all-gather(f32[1,2,2,8]{3,2,1,0:T(2,128)S(1)} %get-tuple-element.106), channel_id=1, replica_groups=mesh['beam'=8,'row'=32] {'row'}, dimensions={0}, use_global_device_ids=true | all-gather | bytes 4224 | tf_op jit(solution)/shard_map/all_gather | solution.py:132
  461.1 47.3 %all_gather.72 = f32[32,2,2,8]{3,2,1,0:T(2,128)S(1)} all-gather(f32[1,2,2,8]{3,2,1,0:T(2,128)S(1)} %get-tuple-element.107), channel_id=1, replica_groups=mesh['beam'=8,'row'=32] {'row'}, dimensions={0}, use_global_device_ids=true | all-gather | bytes 4224 | tf_op jit(solution)/shard_map/all_gather | solution.py:132
  508.9 46.9 %all_gather.77 = f32[32,2,2,8]{3,2,1,0:T(2,128)S(1)} all-gather(f32[1,2,2,8]{3,2,1,0:T(2,128)S(1)} %get-tuple-element.108), channel_id=1, replica_groups=mesh['beam'=8,'row'=32] {'row'}, dimensions={0}, use_global_device_ids=true | all-gather | bytes 4224 | tf_op jit(solution)/shard_map/all_gather | solution.py:132
  556.0 47.3 %all_gather.82 = f32[32,2,2,8]{3,2,1,0:T(2,128)S(1)} all-gather(f32[1,2,2,8]{3,2,1,0:T(2,128)S(1)} %get-tuple-element.109), channel_id=1, replica_groups=mesh['beam'=8,'row'=32] {'row'}, dimensions={0}, use_global_device_ids=true | all-gather | bytes 4224 | tf_op jit(solution)/shard_map/all_gather | solution.py:132
  603.6 12.3 %all_gather.83 = bf16[2,16,8,64]{3,2,0,1:T(8,128)(2,1)S(1)} all-gather(bf16[2,2,8,64]{3,2,0,1:T(8,128)(2,1)S(1)} %copy.375), channel_id=1, replica_groups=mesh['beam'=8,'row'=32] {'beam'}, dimensions={1}, use_global_device_ids=true | all-gather | bytes 36864 | tf_op jit(solution)/shard_map/all_gather | solution.py:139
  616.3 12.7 %all_gather.78 = bf16[2,16,8,64]{3,2,0,1:T(8,128)(2,1)S(1)} all-gather(bf16[2,2,8,64]{3,2,0,1:T(8,128)(2,1)S(1)} %copy.359), channel_id=1, replica_groups=mesh['beam'=8,'row'=32] {'beam'}, dimensions={1}, use_global_device_ids=true | all-gather | bytes 36864 | tf_op jit(solution)/shard_map/all_gather | solution.py:139
  629.3 12.7 %all_gather.73 = bf16[2,16,8,64]{3,2,0,1:T(8,128)(2,1)S(1)} all-gather(bf16[2,2,8,64]{3,2,0,1:T(8,128)(2,1)S(1)} %copy.343), channel_id=1, replica_groups=mesh['beam'=8,'row'=32] {'beam'}, dimensions={1}, use_global_device_ids=true | all-gather | bytes 36864 | tf_op jit(solution)/shard_map/all_gather | solution.py:139
  642.4 12.7 %all_gather.68 = bf16[2,16,8,64]{3,2,0,1:T(8,128)(2,1)S(1)} all-gather(bf16[2,2,8,64]{3,2,0,1:T(8,128)(2,1)S(1)} %copy.327), channel_id=1, replica_groups=mesh['beam'=8,'row'=32] {'beam'}, dimensions={1}, use_global_device_ids=true | all-gather | bytes 36864 | tf_op jit(solution)/shard_map/all_gather | solution.py:139
  656.7 145.0 %all-reduce.7 = (bf16[32,1024]{1,0:T(8,128)(2,1)S(1)}, bf16[32,1024]{1,0:T(8,128)(2,1)S(1)}, bf16[32,1024]{1,0:T(8,128)(2,1)S(1)}, bf16[32,1024]{1,0:T(8,128)(2,1)S(1)}) all-reduce(f32[32,1024]{1,0:T(8,128)S(1)} %convolution_bitcast_fusion.4, ...), channel_id=9, replica_groups=mesh['beam'=8,'row'=32] {'row'}, use_global_device_ids=true, to_apply=%region_35.36.clone | all-reduce | flops 131072 | bytes 786432
  (213 shorter events, 87.6 us)
Async XLA Ops:
  7.2 608.8 %copy-start = (bf16[512,1024]{1,0:T(8,128)(2,1)S(1)}, bf16[512,1024]{1,0:T(8,128)(2,1)}, u32[]{:S(2)}) copy-start(bf16[512,1024]{1,0:T(8,128)(2,1)} %param.25) | copy-start | bytes 3145732
  7.2 115.6 %reduce-scatter.5.cloned.1.call-start = ((), (), s32[]{:S(2)}) async-start(), calls=%async_computation.5 | async-start | bytes 294912 | tf_op jit(solution)/shard_map/reduce_scatter | solution.py:88
  14.0 109.6 %reduce-scatter.7.cloned.1.call-start = ((), (), s32[]{:S(2)}) async-start(), calls=%async_computation.7 | async-start | bytes 294912 | tf_op jit(solution)/shard_map/reduce_scatter | solution.py:88
  15.9 121.6 %reduce-scatter.9.cloned.1.call-start = ((), (), s32[]{:S(2)}) async-start(), calls=%async_computation.9 | async-start | bytes 294912 | tf_op jit(solution)/shard_map/reduce_scatter | solution.py:88
  17.9 133.6 %reduce-scatter.11.cloned.1.call-start = ((), (), s32[]{:S(2)}) async-start(), calls=%async_computation.11 | async-start | bytes 294912 | tf_op jit(solution)/shard_map/reduce_scatter | solution.py:88
  19.9 26.4 %copy-start.6 = (bf16[2,2,3,2,64]{4,3,2,1,0:T(2,128)(2,1)S(1)}, bf16[2,2,3,2,64]{4,3,2,1,0:T(2,128)(2,1)}, u32[]{:S(2)}) copy-start(bf16[2,2,3,2,64]{4,3,2,1,0:T(2,128)(2,1)} %param.28) | copy-start | bytes 9220
  19.9 186.9 %all-gather.5.cloned.1.call-start = ((), (), s32[]{:S(2)}) async-start(), calls=%async_computation.4 | async-start | bytes 9437184 | tf_op jit(solution)/shard_map/all_gather | solution.py:63
  22.2 40.7 %copy-start.7 = (s32[4,2,16]{2,1,0:T(2,128)S(1)}, s32[4,2,16]{2,1,0:T(2,128)}, u32[]{:S(2)}) copy-start(s32[4,2,16]{2,1,0:T(2,128)} %param.29) | copy-start | bytes 1540
  22.2 82.3 %copy-start.4 = (bf16[2,2,8,64,3]{3,2,4,1,0:T(8,128)(2,1)S(1)}, bf16[2,2,8,64,3]{3,2,4,1,0:T(8,128)(2,1)}, u32[]{:S(2)}) copy-start(bf16[2,2,8,64,3]{3,2,4,1,0:T(8,128)(2,1)} %param.27) | copy-start | bytes 36868
  22.2 95.1 %copy-start.12 = (f32[8]{0:T(128)S(1)}, f32[8]{0:T(128)}, u32[]{:S(2)}) copy-start(f32[8]{0:T(128)} %param.22) | copy-start | bytes 100
  22.2 95.3 %copy-start.9 = (f32[8]{0:T(128)S(1)}, f32[8]{0:T(128)}, u32[]{:S(2)}) copy-start(f32[8]{0:T(128)} %param.21) | copy-start | bytes 100
  22.2 95.5 %copy-start.3 = (bf16[4,512]{1,0:T(4,128)(2,1)S(1)}, bf16[4,512]{1,0:T(4,128)(2,1)}, u32[]{:S(2)}) copy-start(bf16[4,512]{1,0:T(4,128)(2,1)} %param.19) | copy-start | bytes 12292
  22.3 248.9 %all-gather.7.cloned.1.call-start = ((), (), s32[]{:S(2)}) async-start(), calls=%async_computation.6 | async-start | bytes 9437184 | tf_op jit(solution)/shard_map/all_gather | solution.py:63
  102.8 15.0 %collective-permute-start = (bf16[2,2,2,64]{3,1,2,0:T(2,128)(2,1)S(1)}, bf16[2,2,2,64]{3,1,2,0:T(2,128)(2,1)S(1)}, u32[]{:S(2)}, u32[]{:S(2)}) collective-permute-start(bf16[2,2,2,64]{3,1,2,0:T(2,128)(2,1)S(1)} %get-tuple-element.105), channel_id=1, source_target_pairs={{0,1},{1,0},{2,3},{3,2},{4,5},{5,4},{6,7},{7,6},{8,9},{9,8},{10,11... | collective-permute-start | bytes 3080 | tf_op jit(solution)/shard_map/ppermute | solution.py:13
  117.8 4.9 collective-permute-start.1
  218.6 117.1 %all-gather.9.cloned.1.call-start = ((), (), s32[]{:S(2)}) async-start(), calls=%async_computation.8 | async-start | bytes 9437184 | tf_op jit(solution)/shard_map/all_gather | solution.py:63
  218.6 3.7 collective-permute-start.2
  222.4 4.5 collective-permute-start.3
  283.0 117.1 %all-gather.11.cloned.1.call-start = ((), (), s32[]{:S(2)}) async-start(), calls=%async_computation.10 | async-start | bytes 9437184 | tf_op jit(solution)/shard_map/all_gather | solution.py:63
  283.1 3.8 collective-permute-start.4
  287.0 4.5 collective-permute-start.5
  347.5 3.7 collective-permute-start.6
  351.2 4.5 collective-permute-start.7
  400.1 10.8 %copy-start.10 = (f32[8]{0:T(128)S(1)}, f32[8]{0:T(128)}, u32[]{:S(2)}) copy-start(f32[8]{0:T(128)} %param.23) | copy-start | bytes 100
  (6 other events, 31.7 us)
Sparse Core Ops, SparseCore 0:
  14.1 30.9 reduce-scatter.4
  47.8 31.9 reduce-scatter.6
  82.3 31.9 reduce-scatter.8
  116.8 32.1 reduce-scatter.10
  151.3 55.4 all-gather.4
  218.7 52.4 all-gather.6
  283.1 52.4 all-gather.8
  347.6 52.4 all-gather.10
